TPU v7x, 256 devices: a whole 4x4x8 slice. The times are simulated.
256 devices in a mesh: grp: 16 (over y, z_hi), blk: 16 (over x, z_lo, core).
Axes of the slice: x: 4, y: 4, z: 8 (z_hi: 4, z_lo: 2; z = z_hi * 2 + z_lo), core: 2. Of those that a mesh axis runs over, the one named last changes fastest.
Arguments:
- feats: bfloat16 [196608, 128], P(('grp', 'blk')), may hold values from -6 to 6
- proj: bfloat16 [128, 512], replicated, may hold values from -0.5 to 0.5
- att_src: float32 [8, 64], replicated
- target_attention_vector: float32 [8, 64], replicated
- edge_mask: int32 [196608, 5, 768], P(('grp', 'blk')), may hold values from 0 to 1
- send_rows: int32 [256, 16, 32], P(('grp', 'blk')), may hold values from 0 to 767
- send_count: int32 [16, 16, 16], P(None, 'blk', 'grp'), may hold values from 0 to 32, as said below
- bound_mask: int32 [196608, 512], P(('grp', 'blk')), may hold values 0 or 1
Outputs:
- node_out: bfloat16 [196608, 512], P(('grp', 'blk'))
Inputs may be any that keep to these rules, and one draw needn't show every extreme that they name: `send_count`: a group sends nothing to itself; every device fills all 32 slots for some other group.
All inputs are finite; a program needn't handle non-finite values. No bound on the sum of `bound_mask` on one device may be relied on, other than what follows from the above.
Results may differ from a plain program's by a relative error of at most 0.0095.
Values may be sent and summed in bfloat16 or wider, within the bound.
No kernel may reach another device: no remote copies, remote signals or barrier semaphores. Data moves between devices by JAX's collectives and lax.ppermute only.
A program may use at most 64 MiB of HBM per device.

v0:
```python
import functools

import jax
import jax.numpy as jnp
from jax import lax
from jax.experimental import pallas as pl
from jax.experimental.pallas import tpu as pltpu
from jax.sharding import PartitionSpec as P

HEADS = 8
HEAD_DIM = 64
HOPS = 5
LANES = 128
ROWS = 80
TILE = 256
SPAN = 60.0
F32 = jnp.float32
BF16 = jnp.bfloat16
NT = (((1,), (1,)), ((), ()))
NN = (((1,), (0,)), ((), ()))
WHOLE = pl.BlockSpec(memory_space=pltpu.VMEM)


def mm(a, b, dims=NN):
    return lax.dot_general(a, b, dims, preferred_element_type=F32)


def in_hbm(x):
    return pltpu.with_memory_space_constraint(x, pltpu.HBM)


def iota(shape, axis):
    return lax.broadcasted_iota(jnp.int32, shape, axis)


def pieces(x):
    hi = x.astype(BF16)
    rest = x - hi.astype(F32)
    mid = rest.astype(BF16)
    low = (rest - mid.astype(F32)).astype(BF16)
    return hi, mid, low


def pick_kernel(rows_ref, feats_ref, out_ref, chosen):
    groups, cap = rows_ref.shape
    count = feats_ref.shape[0]
    rows = rows_ref[...].astype(F32)
    high = jnp.floor(rows * (1.0 / 256.0))
    low = rows - 256.0 * high
    unit = jnp.where(iota((cap, cap), 0) == iota((cap, cap), 1), 1.0, 0.0).astype(BF16)
    turned = mm(unit, high.astype(BF16), NT) * 256.0 + mm(unit, low.astype(BF16), NT)
    turned = turned.astype(jnp.int32)
    lane = iota((cap, count), 1)
    for p in range(groups):
        hit = lane == turned[:, p : p + 1]
        chosen[p * cap : (p + 1) * cap, :] = jnp.where(hit, 1.0, 0.0).astype(BF16)
    out_ref[...] = mm(chosen[...], feats_ref[...]).astype(BF16)


def pick_rows(send_rows, feats):
    groups, cap = send_rows.shape
    return pl.pallas_call(
        pick_kernel,
        out_shape=jax.ShapeDtypeStruct((groups * cap, feats.shape[1]), BF16),
        scratch_shapes=[pltpu.VMEM((groups * cap, feats.shape[0]), BF16)],
        name="pick_rows",
    )(send_rows, feats)


def spread_heads(vector):
    width = HEADS * HEAD_DIM
    tiler = jnp.where(iota((HEAD_DIM, width), 1) % HEAD_DIM == iota((HEAD_DIM, width), 0), 1.0, 0.0).astype(BF16)
    own = iota((HEADS, width), 1) // HEAD_DIM == iota((HEADS, width), 0)
    parts = [jnp.where(own, mm(p, tiler), 0.0) for p in pieces(vector)]
    parts.append(jnp.zeros((HEADS, width), F32))
    return jnp.concatenate(parts, axis=0).astype(BF16)


def logits(spread, turned):
    s = mm(spread, turned)
    return s[0:HEADS] + s[HEADS : 2 * HEADS] + s[2 * HEADS : 3 * HEADS]


def steps(s):
    return jnp.exp(0.2 * s), jnp.exp(0.8 * s).T.astype(BF16)


def prepare(h, turned, flat, steep, table, rise):
    size = flat.shape[1]
    tail = jnp.broadcast_to(flat[h : h + 1], (ROWS - HEAD_DIM, size)).astype(BF16)
    part = turned[h * HEAD_DIM : (h + 1) * HEAD_DIM].reshape(HEAD_DIM // 16, 16, size) * tail[None]
    part = part.reshape(HEAD_DIM, size)
    for t in range(size // LANES):
        lanes = slice(t * LANES, (t + 1) * LANES)
        table[h, t, 0:HEAD_DIM, :] = part[:, lanes]
        table[h, t, HEAD_DIM:ROWS, :] = tail[:, lanes]
    rise[h] = jnp.broadcast_to(steep[:, h : h + 1], (size, LANES))


def weighted(h, planes, table, rise, ratio, mask):
    size = rise.shape[1]
    steep = rise[h].reshape(size // 16, 16, LANES)
    left = jnp.concatenate([table[h, t] for t in range(size // LANES)], axis=1)
    cols = []
    for plane in planes:
        w = jnp.maximum(steep, ratio[h, plane][None]) * mask[plane].reshape(size // 16, 16, LANES)
        cols.append(w.reshape(size, LANES))
    return mm(left, jnp.concatenate(cols, axis=1))


def elu(x):
    small = x * (1.0 + 0.5 * x)
    low = jnp.where(x > -1e-3, small, jnp.exp(jnp.minimum(x, 0.0)) - 1.0)
    return jnp.where(x > 0, x, low)


def largest(*scores):
    worst = functools.reduce(jnp.maximum, [jnp.max(jnp.abs(s), axis=1, keepdims=True) for s in scores])
    return jnp.broadcast_to(worst, (HEADS, LANES))


def turned_tile(m, diagonal):
    m = m.astype(F32)
    if diagonal is not None:
        m = jnp.where(iota(m.shape, 0) == iota(m.shape, 1) + diagonal, 1.0, m)
    return m.astype(BF16).T


def turn_kernel(count_ref, edge_hbm, bound_hbm, edge_out, bound_out, edge, bound, edge_t, bound_t, sems, sent):
    nodes, slots = bound.shape
    hops = edge.shape[0]
    half = nodes // 2
    planes = nodes // LANES
    cap = slots // count_ref.shape[0]
    parts = [(hop, i) for hop in range(hops) for i in range(2)]
    copies, sends = [], []
    for k, (hop, i) in enumerate(parts):
        rows, some = pl.ds(i * half, half), pl.ds(i * planes // 2, planes // 2)
        copies.append(pltpu.make_async_copy(edge_hbm.at[hop, rows, :], edge.at[hop, rows, :], sems.at[k]))
        sends.append(pltpu.make_async_copy(edge_t.at[hop, some], edge_out.at[hop, some], sent.at[k]))
    copies.append(pltpu.make_async_copy(bound_hbm, bound, sems.at[2 * hops]))
    sends.append(pltpu.make_async_copy(bound_t, bound_out, sent.at[2 * hops]))
    for copy in copies:
        copy.start()
    lane = iota((1, slots), 1)
    live = jnp.zeros((1, slots), F32)
    for p in range(count_ref.shape[0]):
        live = jnp.where((lane // cap == p) & (lane % cap < count_ref[p]), 1.0, live)
    for k, (hop, i) in enumerate(parts):
        copies[k].wait()
        for plane in range(i * planes // 2, (i + 1) * planes // 2):
            rows = slice(plane * LANES, (plane + 1) * LANES)
            for t in range(planes):
                lanes = slice(t * LANES, (t + 1) * LANES)
                edge_t[hop, plane, lanes, :] = turned_tile(edge[hop, rows, lanes], 0 if hop == 0 and t == plane else None)
        sends[k].start()
    copies[2 * hops].wait()
    for plane in range(planes):
        m = bound[plane * LANES : (plane + 1) * LANES, :].astype(F32) * live
        for t in range(slots // LANES):
            lanes = slice(t * LANES, (t + 1) * LANES)
            bound_t[plane, lanes, :] = turned_tile(m[:, lanes], None)
    sends[2 * hops].start()
    for send in sends:
        send.wait()


def turn_masks(counts, edges, bound):
    hops, nodes = edges.shape[0], edges.shape[1]
    slots = bound.shape[1]
    planes = nodes // LANES
    far = pl.BlockSpec(memory_space=pl.ANY)
    edge_t, bound_t = pl.pallas_call(
        turn_kernel,
        out_shape=(
            jax.ShapeDtypeStruct((hops, planes, nodes, LANES), BF16),
            jax.ShapeDtypeStruct((planes, slots, LANES), BF16),
        ),
        in_specs=[pl.BlockSpec(memory_space=pltpu.SMEM), far, far],
        out_specs=(pl.BlockSpec(memory_space=pltpu.HBM),) * 2,
        scratch_shapes=[
            pltpu.VMEM((hops, nodes, nodes), jnp.int32),
            pltpu.VMEM((nodes, slots), jnp.int32),
            pltpu.VMEM((hops, planes, nodes, LANES), BF16),
            pltpu.VMEM((planes, slots, LANES), BF16),
            pltpu.SemaphoreType.DMA((2 * hops + 1,)),
            pltpu.SemaphoreType.DMA((2 * hops + 1,)),
        ],
        compiler_params=pltpu.CompilerParams(vmem_limit_bytes=58 << 20),
        name="turn_masks",
    )(counts, in_hbm(edges), in_hbm(bound))
    return in_hbm(edge_t), in_hbm(bound_t)


def scratch(size, nodes, copies):
    planes = nodes // LANES
    return (
        *[pltpu.VMEM((HEADS, size // LANES, ROWS, LANES), BF16)] * copies,
        *[pltpu.VMEM((HEADS, size, LANES), BF16)] * copies,
        *[pltpu.VMEM((planes, size, LANES), BF16)] * copies,
        pltpu.VMEM((HEADS, planes, 16, LANES), BF16),
    )


def spread_ratio(d, ratio):
    r = jnp.exp(-0.8 * d)
    for h in range(HEADS):
        for p in range(d.shape[1] // LANES):
            row = r[h : h + 1, p * LANES : (p + 1) * LANES]
            ratio[h, p] = jnp.broadcast_to(row, (16, LANES)).astype(BF16)


def blocks_kernel(
    x0, x1, x2, x3, x4, proj_ref, src_ref, dst_ref, mask_hbm, acc_ref, dst_out, worst_ref, landed, sems
):
    nodes = x0.shape[0]
    planes = nodes // LANES
    per = TILE // LANES
    xs = (x0, x1, x2, x3, x4)
    copies = [pltpu.make_async_copy(mask_hbm.at[b], landed.at[b], sems.at[b]) for b in range(HOPS)]
    for copy in copies:
        copy.start()

    def body(table_a, table_b, rise_a, rise_b, mask_a, mask_b, ratio):
        tables, rises, masks = (table_a, table_b), (rise_a, rise_b), (mask_a, mask_b)
        proj_t = proj_ref[...].T
        spread = spread_heads(src_ref[...])

        def begin(b):
            turned = mm(proj_t, xs[b][...], NT).astype(BF16)
            return turned, logits(spread, turned)

        turned, s = begin(0)
        d = logits(spread_heads(dst_ref[...]), turned)
        dst_out[...] = d
        spread_ratio(d, ratio)
        worst = largest(s, d)
        flat, steep = steps(s)
        for h in range(HEADS):
            prepare(h, turned, flat, steep, table_a, rise_a)
        copies[0].wait()
        for p in range(planes):
            mask_a[p] = landed[0, p]
        for b in range(HOPS):
            now, later = b % 2, (b + 1) % 2
            if b + 1 < HOPS:
                turned, s = begin(b + 1)
                worst = jnp.maximum(worst, largest(s))
                flat, steep = steps(s)
                copies[b + 1].wait()
                for p in range(planes):
                    masks[later][p] = landed[b + 1, p]
            for h in range(HEADS):
                if b + 1 < HOPS:
                    prepare(h, turned, flat, steep, tables[later], rises[later])
                for i in range(nodes // TILE):
                    lanes = slice(i * TILE, (i + 1) * TILE)
                    part = weighted(h, range(i * per, (i + 1) * per), tables[now], rises[now], ratio, masks[now])
                    acc_ref[h, :, lanes] = part if b == 0 else acc_ref[h, :, lanes] + part
        worst_ref[...] = worst

    pl.run_scoped(body, *scratch(nodes, nodes, 2))


def node_blocks(blocks, proj, att_src, att_dst, mask):
    nodes = blocks[0].shape[0]
    shape = jax.ShapeDtypeStruct
    return pl.pallas_call(
        blocks_kernel,
        out_shape=(shape((HEADS, ROWS, nodes), F32), shape((HEADS, nodes), F32), shape((HEADS, LANES), F32)),
        in_specs=[WHOLE] * 8 + [pl.BlockSpec(memory_space=pl.ANY)],
        out_specs=(WHOLE,) * 3,
        scratch_shapes=[pltpu.VMEM(mask.shape, BF16), pltpu.SemaphoreType.DMA((HOPS,))],
        compiler_params=pltpu.CompilerParams(vmem_limit_bytes=28 << 20),
        name="node_blocks",
    )(*blocks, proj, att_src, att_dst, mask)


def last_kernel(
    x0, x1, x2, x3, x4, xs, proj_ref, src_ref, dst_ref, worst_a, acc_in, slot_hbm, edge_any,
    out_ref,
    mask_ref, sem, turned_out, raw, hidden, cols, masks, tops, sums,
):
    nodes = x0.shape[0]
    planes = nodes // LANES
    per = TILE // LANES
    arrival = pltpu.make_async_copy(slot_hbm, mask_ref, sem)
    arrival.start()
    turned_slots = mm(proj_ref[...].T, xs[...], NT).astype(BF16)
    slot_scores = logits(spread_heads(src_ref[...]), turned_slots)
    worst = jnp.max(jnp.maximum(worst_a[...], largest(slot_scores)))
    arrival.wait()

    def finish(h, acc):
        o = acc[0:HEAD_DIM] * (1.0 / acc[HEAD_DIM : HEAD_DIM + 1])
        turned_out[h * HEAD_DIM : (h + 1) * HEAD_DIM, :] = elu(o)

    @pl.when(worst <= SPAN)
    def _():
        def body(table, rise, mask, ratio):
            spread_ratio(dst_ref[...], ratio)
            flat, steep = steps(slot_scores)
            for p in range(planes):
                mask[p] = mask_ref[p]
            for h in range(HEADS):
                prepare(h, turned_slots, flat, steep, table, rise)
            for i in range(nodes // TILE):
                lanes = slice(i * TILE, (i + 1) * TILE)
                for h in range(HEADS):
                    part = weighted(h, range(i * per, (i + 1) * per), table, rise, ratio, mask)
                    finish(h, acc_in[h, :, lanes] + part)
                out_ref[lanes, :] = turned_out[...].T.astype(BF16)

        pl.run_scoped(body, *scratch(xs.shape[0], nodes, 1))

    @pl.when(jnp.logical_not(worst <= SPAN))
    def _():
        tops[...] = jnp.full(tops.shape, -jnp.inf, F32)
        sums[...] = jnp.zeros(sums.shape, F32)
        for second in (False, True):
            for b, x in enumerate((x0, x1, x2, x3, x4, xs)):
                size = x.shape[0]
                if b == HOPS:
                    masks[:, 0:size, :] = mask_ref[...]
                else:

                    def turn(p, carry):
                        pltpu.sync_copy(edge_any.at[b, pl.ds(pl.multiple_of(p * LANES, LANES), LANES), :], raw)
                        for t in range(planes):
                            lanes = slice(t * LANES, (t + 1) * LANES)
                            diagonal = (t - p) * LANES if b == 0 else None
                            masks[p, lanes, :] = turned_tile(raw[:, lanes], diagonal)
                        return carry

                    lax.fori_loop(0, planes, turn, 0)
                turned = mm(proj_ref[...].T, x[...], NT).astype(BF16)
                cols[0:size] = logits(spread_heads(src_ref[...]), turned).T
                for h in range(HEADS):
                    hidden[h, 0:HEAD_DIM, 0:size] = turned[h * HEAD_DIM : (h + 1) * HEAD_DIM]
                    hidden[h, HEAD_DIM:ROWS, 0:size] = jnp.ones((ROWS - HEAD_DIM, size), BF16)

                def one(i, carry):
                    h, p = i // planes, i % planes
                    lanes = pl.ds(pl.multiple_of(p * LANES, LANES), LANES)
                    c = cols[0:size]
                    s = jnp.sum(jnp.where(iota(c.shape, 1) == h, c, 0.0), axis=1, keepdims=True)
                    d = dst_ref[:, lanes]
                    v = s + jnp.sum(jnp.where(iota(d.shape, 0) == h, d, 0.0), axis=0, keepdims=True)
                    v = jnp.maximum(v, 0.2 * v)
                    v = jnp.where(masks[p, 0:size].astype(F32) > 0, v, -jnp.inf)
                    if second:
                        w = jnp.exp(v - tops[h, 0:1, lanes]).astype(BF16)
                        sums[h, :, lanes] += mm(hidden[h, :, 0:size], w)
                    else:
                        tops[h, :, lanes] = jnp.maximum(tops[h, :, lanes], jnp.max(v, axis=0, keepdims=True))
                    return carry

                lax.fori_loop(0, HEADS * planes, one, 0)
        for i in range(nodes // TILE):
            lanes = slice(i * TILE, (i + 1) * TILE)
            for h in range(HEADS):
                finish(h, sums[h, :, lanes])
            out_ref[lanes, :] = turned_out[...].T.astype(BF16)


def last_block(blocks, slots, proj, att_src, dst, worst, acc, bound, edges):
    nodes = acc.shape[2]
    width = proj.shape[1]
    return pl.pallas_call(
        last_kernel,
        out_shape=jax.ShapeDtypeStruct((nodes, width), BF16),
        in_specs=[WHOLE] * 11 + [pl.BlockSpec(memory_space=pl.ANY)] * 2,
        out_specs=WHOLE,
        scratch_shapes=[
            pltpu.VMEM(bound.shape, BF16),
            pltpu.SemaphoreType.DMA,
            pltpu.VMEM((width, TILE), F32),
            pltpu.VMEM((LANES, nodes), jnp.int32),
            pltpu.VMEM((HEADS, ROWS, nodes), BF16),
            pltpu.VMEM((nodes, HEADS), F32),
            pltpu.VMEM((nodes // LANES, nodes, LANES), BF16),
            pltpu.VMEM((HEADS, 8, nodes), F32),
            pltpu.VMEM((HEADS, ROWS, nodes), F32),
        ],
        compiler_params=pltpu.CompilerParams(vmem_limit_bytes=24 << 20),
        name="last_block",
    )(*blocks, slots, proj, att_src, dst, worst, acc, bound, edges)


def attend(counts, blocks, slots, proj, att_src, att_dst, edges, bound):
    mask, bound = turn_masks(counts, edges, bound)
    acc, dst, worst = node_blocks(blocks, proj, att_src, att_dst, mask)
    return last_block(blocks, slots, proj, att_src, dst, worst, acc, bound, in_hbm(edges))


def passed_along(block, axis, distance):
    devices = range(lax.axis_size(axis))
    return lax.ppermute(block, axis, [((i - distance) % len(devices), i) for i in devices])


def other_core(block):
    return lax.ppermute(block, "blk", [(i, i ^ 1) for i in range(lax.axis_size("blk"))])


def local(feats, proj, att_src, att_dst, edge_mask, send_rows, send_count, bound_mask):
    edges = in_hbm(jnp.transpose(edge_mask, (1, 0, 2)))
    two = passed_along(feats, "blk", 2)
    four = passed_along(feats, "blk", 4)
    outgoing = pick_rows(send_rows[0], feats)
    arrived = lax.all_to_all(outgoing, "grp", split_axis=0, concat_axis=0, tiled=True)
    mask, bound = turn_masks(in_hbm(send_count.reshape(-1)), edges, bound_mask)
    two, four, mask, _ = lax.optimization_barrier((two, four, mask, outgoing))
    mask = in_hbm(mask)
    second = lax.axis_index("blk") % 2 == 1
    outer = other_core(jnp.where(second, four, feats))
    inner = other_core(two)
    one = jnp.where(second, outer, inner)
    three = jnp.where(second, inner, outer)
    blocks = (feats, one, two, three, four)
    acc, dst, worst = node_blocks(blocks, proj, att_src, att_dst, mask)
    return last_block(blocks, arrived, proj, att_src, dst, worst, acc, bound, edges)


def solution(mesh):
    in_specs = (
        P(("grp", "blk"), None),
        P(),
        P(),
        P(),
        P(("grp", "blk"), None, None),
        P(("grp", "blk"), None, None),
        P(None, "blk", "grp"),
        P(("grp", "blk"), None),
    )
    out_specs = P(("grp", "blk"), None)
    return jax.shard_map(local, mesh=mesh, in_specs=in_specs, out_specs=out_specs, check_vma=False)
```

profile of v0, /device:TPU:1, one launch (start us, length us, event | category | flops | bytes accessed | tf_op | source)
XLA Modules:
  0.0 267.3 jit_solution(9362408946682057498)
XLA Ops:
  0.0 2.0 collective-permute-start.1
  2.0 1.6 collective-permute-start
  3.7 2.2 pick_rows.1
  5.9 0.0 copy-start
  5.9 0.0 copy-start.1
  5.9 0.0 copy-start.2
  5.9 0.0 copy-start.3
  5.9 8.9 %turn_masks.1 = (bf16[5,6,768,128]{3,2,1,0:T(8,128)(2,1)}, bf16[6,512,128]{2,1,0:T(8,128)(2,1)}) custom-call(s32[16]{0:T(128)} %bitcast.9, s32[5,768,768]{2,1,0:T(8,128)} %bitcast.6, s32[768,512]{1,0:T(8,128)} %bound_hbm.1), custom_call_target="tpu_custom_call" | custom-call | tf_op jit(solution)/shard_map/turn_masks/pallas_call | solution.py:173
  14.8 0.0 collective-permute-done.1.x4
  14.8 0.0 collective-permute-done.x2
  14.8 0.0 copy-done
  14.9 1.3 collective-permute-start.2
  16.2 0.1 collective-permute-start.3
  16.3 10.0 %all-to-all-start = ((bf16[16,32,128]{2,1,0:T(8,128)(2,1)}), bf16[16,32,128]{2,1,0:T(8,128)(2,1)S(1)}, u32[]{:S(2)}, u32[]{:S(2)}) async-start(bf16[16,32,128]{2,1,0:T(8,128)(2,1)} %bitcast.3), calls=%async_computation | async-start | bytes 262144 | tf_op jit(solution)/shard_map/all_to_all | solution.py:410
  26.4 0.0 collective-permute-done.2
  26.4 0.0 collective-permute-done.3
  26.4 0.0 copy-done.1
  26.4 0.0 copy-done.2
  26.4 0.0 copy-done.3
  26.4 11.5 %node_blocks.1 = (f32[8,80,768]{2,1,0:T(8,128)S(1)}, f32[8,768]{1,0:T(8,128)S(1)}, f32[8,128]{1,0:T(8,128)S(1)}) custom-call(bf16[768,128]{1,0:T(8,128)(2,1)S(1)} %copy-done, bf16[768,128]{1,0:T(8,128)(2,1)S(1)} %get-tuple-element.22.x1, bf16[768,128]{1,0:T(8,128)(2,1)S(1)} %collective-permute-done.x2, bf16[768,128]{1,0:T(8,128)(2,1)S(1)} %get-tuple-element.21.x3, ...), custom_call_target="tpu_custom_call" | custom-call | tf_op jit(solution)/shard_map/node_blocks/pallas_call | solution.py:268
  38.0 0.0 all-to-all-done
  38.0 229.1 %last_block.1 = bf16[768,512]{1,0:T(8,128)(2,1)} custom-call(bf16[768,128]{1,0:T(8,128)(2,1)S(1)} %copy-done, bf16[768,128]{1,0:T(8,128)(2,1)S(1)} %get-tuple-element.22.x1, bf16[768,128]{1,0:T(8,128)(2,1)S(1)} %collective-permute-done.x2, bf16[768,128]{1,0:T(8,128)(2,1)S(1)} %get-tuple-element.21.x3, bf16[768,128]{1,0:T(8,128)(2,1)S(1)} %collective-permute-done.1.x4, ...), custom_call_target="tpu_custom_call" | custom-call | tf_op jit(solution)/shard_map/last_block/pallas_call | solution.py:369
  (2 shorter events, 0.1 us)
Async XLA Ops:
  0.0 14.8 %collective-permute-start.1 = (bf16[768,128]{1,0:T(8,128)(2,1)}, bf16[768,128]{1,0:T(8,128)(2,1)S(1)}, u32[]{:S(2)}, u32[]{:S(2)}) collective-permute-start(bf16[768,128]{1,0:T(8,128)(2,1)} %x0.3), channel_id=1, source_target_pairs={{12,0},{13,1},{14,2},{15,3},{0,4},{1,5},{2,6},{3,7},{4,8},{5,9},{6... | collective-permute-start | bytes 589832 | tf_op jit(solution)/shard_map/ppermute | solution.py:398
  2.0 12.8 %collective-permute-start = (bf16[768,128]{1,0:T(8,128)(2,1)}, bf16[768,128]{1,0:T(8,128)(2,1)S(1)}, u32[]{:S(2)}, u32[]{:S(2)}) collective-permute-start(bf16[768,128]{1,0:T(8,128)(2,1)} %x0.3), channel_id=1, source_target_pairs={{14,0},{15,1},{0,2},{1,3},{2,4},{3,5},{4,6},{5,7},{6,8},{7,9},{8,1... | collective-permute-start | bytes 589832 | tf_op jit(solution)/shard_map/ppermute | solution.py:398
  5.9 9.0 %copy-start = (bf16[768,128]{1,0:T(8,128)(2,1)S(1)}, bf16[768,128]{1,0:T(8,128)(2,1)}, u32[]{:S(2)}) copy-start(bf16[768,128]{1,0:T(8,128)(2,1)} %x0.3) | copy-start | bytes 589828
  5.9 20.5 %copy-start.1 = (bf16[128,512]{1,0:T(8,128)(2,1)S(1)}, bf16[128,512]{1,0:T(8,128)(2,1)}, u32[]{:S(2)}) copy-start(bf16[128,512]{1,0:T(8,128)(2,1)} %proj_ref.3) | copy-start | bytes 393220
  5.9 20.5 %copy-start.2 = (f32[8,64]{1,0:T(8,128)S(1)}, f32[8,64]{1,0:T(8,128)}, u32[]{:S(2)}) copy-start(f32[8,64]{1,0:T(8,128)} %src_ref.3) | copy-start | bytes 6148
  5.9 20.5 %copy-start.3 = (f32[8,64]{1,0:T(8,128)S(1)}, f32[8,64]{1,0:T(8,128)}, u32[]{:S(2)}) copy-start(f32[8,64]{1,0:T(8,128)} %dst_ref.1) | copy-start | bytes 6148
  14.9 11.5 %collective-permute-start.2 = (bf16[768,128]{1,0:T(8,128)(2,1)S(1)}, bf16[768,128]{1,0:T(8,128)(2,1)S(1)}, u32[]{:S(2)}, u32[]{:S(2)}) collective-permute-start(bf16[768,128]{1,0:T(8,128)(2,1)S(1)} %broadcast_select_fusion.2), channel_id=1, source_target_pairs={{0,1},{1,0},{2,3},{3,2},{4,5},{5,4},{6,7},{7,6},{8,9},{9,8},{10,11... | collective-permute-start | bytes 589832 | tf_op jit(solution)/shard_map/ppermute | solution.py:402
  16.2 10.2 %collective-permute-start.3 = (bf16[768,128]{1,0:T(8,128)(2,1)S(1)}, bf16[768,128]{1,0:T(8,128)(2,1)S(1)}, u32[]{:S(2)}, u32[]{:S(2)}) collective-permute-start(bf16[768,128]{1,0:T(8,128)(2,1)S(1)} %collective-permute-done.x2), channel_id=1, source_target_pairs={{0,1},{1,0},{2,3},{3,2},{4,5},{5,4},{6,7},{7,6},{8,9},{9,8},{10,11... | collective-permute-start | bytes 589832 | tf_op jit(solution)/shard_map/ppermute | solution.py:402
  16.3 21.7 %all-to-all-start = ((bf16[16,32,128]{2,1,0:T(8,128)(2,1)}), bf16[16,32,128]{2,1,0:T(8,128)(2,1)S(1)}, u32[]{:S(2)}, u32[]{:S(2)}) async-start(bf16[16,32,128]{2,1,0:T(8,128)(2,1)} %bitcast.3), calls=%async_computation | async-start | bytes 262144 | tf_op jit(solution)/shard_map/all_to_all | solution.py:410
where the time goes:
time: 270 us; the launch traced here: 267 us
  Pallas kernels  252 us (93%)
  starting transfers between devices  15.1 us (6%)
    pallas_call x1, Pallas kernels, last_block(): pl.pallas_call(last_kernel, out_shape=jax.ShapeDtypeStruct((nodes, width)...  229 us
    pallas_call x1, Pallas kernels, node_blocks(): pl.pallas_call(blocks_kernel, out_shape=(shape((HEADS, ROWS, nodes), F32)...  11.5 us
    all_to_all x1, starting transfers between devices, local(): lax.all_to_all(outgoing, 'grp', split_axis=0, concat_axis=0, tiled=True)  10 us
    pallas_call x1, Pallas kernels, turn_masks(): pl.pallas_call(turn_kernel, out_shape=(jax.ShapeDtypeStruct((hops, planes...  8.92 us
  transfers between devices with their start and end apart: 5, of which 0 were waited for; matrix products, arithmetic and copies ran while one was open for 0% of the time, Pallas kernels for 8%

commit v1 on v0

--- a/solution.py
+++ b/solution.py
@@ -13,6 +13,7 @@
 LANES = 128
 ROWS = 80
 TILE = 256
+EARLY = 3
 SPAN = 60.0
 F32 = jnp.float32
 BF16 = jnp.bfloat16
@@ -166,7 +167,7 @@
 
 
 def turn_masks(counts, edges, bound):
-    hops, nodes = edges.shape[0], edges.shape[1]
+    hops, nodes = EARLY, edges.shape[1]
     slots = bound.shape[1]
     planes = nodes // LANES
     far = pl.BlockSpec(memory_space=pl.ANY)
@@ -211,13 +212,18 @@
 
 
 def blocks_kernel(
-    x0, x1, x2, x3, x4, proj_ref, src_ref, dst_ref, mask_hbm, acc_ref, dst_out, worst_ref, landed, sems
+    x0, x1, x2, x3, x4, proj_ref, src_ref, dst_ref, mask_hbm, edge_hbm,
+    acc_ref, dst_out, worst_ref, landed, raw, sems
 ):
     nodes = x0.shape[0]
     planes = nodes // LANES
     per = TILE // LANES
     xs = (x0, x1, x2, x3, x4)
-    copies = [pltpu.make_async_copy(mask_hbm.at[b], landed.at[b], sems.at[b]) for b in range(HOPS)]
+    copies = [pltpu.make_async_copy(mask_hbm.at[b], landed.at[b], sems.at[b]) for b in range(EARLY)]
+    for b in range(EARLY, HOPS):
+        copies.append(pltpu.make_async_copy(edge_hbm.at[b], raw.at[b - EARLY], sems.at[b]))
+    tiles = [(plane, t) for plane in range(planes) for t in range(planes)]
+    share = -(-len(tiles) // HEADS)
     for copy in copies:
         copy.start()
 
@@ -248,11 +254,17 @@
                 worst = jnp.maximum(worst, largest(s))
                 flat, steep = steps(s)
                 copies[b + 1].wait()
-                for p in range(planes):
-                    masks[later][p] = landed[b + 1, p]
+                if b + 1 < EARLY:
+                    for p in range(planes):
+                        masks[later][p] = landed[b + 1, p]
             for h in range(HEADS):
                 if b + 1 < HOPS:
                     prepare(h, turned, flat, steep, tables[later], rises[later])
+                    if b + 1 >= EARLY:
+                        for plane, t in tiles[h * share : (h + 1) * share]:
+                            cut = slice(t * LANES, (t + 1) * LANES)
+                            tile = raw[b + 1 - EARLY, plane * LANES : (plane + 1) * LANES, cut]
+                            masks[later][plane, cut, :] = turned_tile(tile, None)
                 for i in range(nodes // TILE):
                     lanes = slice(i * TILE, (i + 1) * TILE)
                     part = weighted(h, range(i * per, (i + 1) * per), tables[now], rises[now], ratio, masks[now])
@@ -262,18 +274,22 @@
     pl.run_scoped(body, *scratch(nodes, nodes, 2))
 
 
-def node_blocks(blocks, proj, att_src, att_dst, mask):
+def node_blocks(blocks, proj, att_src, att_dst, mask, edges):
     nodes = blocks[0].shape[0]
     shape = jax.ShapeDtypeStruct
     return pl.pallas_call(
         blocks_kernel,
         out_shape=(shape((HEADS, ROWS, nodes), F32), shape((HEADS, nodes), F32), shape((HEADS, LANES), F32)),
-        in_specs=[WHOLE] * 8 + [pl.BlockSpec(memory_space=pl.ANY)],
+        in_specs=[WHOLE] * 8 + [pl.BlockSpec(memory_space=pl.ANY)] * 2,
         out_specs=(WHOLE,) * 3,
-        scratch_shapes=[pltpu.VMEM(mask.shape, BF16), pltpu.SemaphoreType.DMA((HOPS,))],
-        compiler_params=pltpu.CompilerParams(vmem_limit_bytes=28 << 20),
+        scratch_shapes=[
+            pltpu.VMEM(mask.shape, BF16),
+            pltpu.VMEM((HOPS - EARLY, nodes, nodes), jnp.int32),
+            pltpu.SemaphoreType.DMA((HOPS,)),
+        ],
+        compiler_params=pltpu.CompilerParams(vmem_limit_bytes=30 << 20),
         name="node_blocks",
-    )(*blocks, proj, att_src, att_dst, mask)
+    )(*blocks, proj, att_src, att_dst, mask, in_hbm(edges))
 
 
 def last_kernel(
@@ -389,7 +405,7 @@
 
 def attend(counts, blocks, slots, proj, att_src, att_dst, edges, bound):
     mask, bound = turn_masks(counts, edges, bound)
-    acc, dst, worst = node_blocks(blocks, proj, att_src, att_dst, mask)
+    acc, dst, worst = node_blocks(blocks, proj, att_src, att_dst, mask, edges)
     return last_block(blocks, slots, proj, att_src, dst, worst, acc, bound, in_hbm(edges))
 
 
@@ -417,7 +433,7 @@
     one = jnp.where(second, outer, inner)
     three = jnp.where(second, inner, outer)
     blocks = (feats, one, two, three, four)
-    acc, dst, worst = node_blocks(blocks, proj, att_src, att_dst, mask)
+    acc, dst, worst = node_blocks(blocks, proj, att_src, att_dst, mask, edges)
     return last_block(blocks, arrived, proj, att_src, dst, worst, acc, bound, edges)
 
 

time: 270 us -> 268 us (level)
  Pallas kernels: 252 us -> 249 us
where the time goes in v1:
time: 268 us; the launch traced here: 266 us
  Pallas kernels  249 us (93%)
  starting transfers between devices  16.1 us (6%)
    pallas_call x1, Pallas kernels, last_block(): pl.pallas_call(last_kernel, out_shape=jax.ShapeDtypeStruct((nodes, width)...  229 us
    pallas_call x1, Pallas kernels, node_blocks(): pl.pallas_call(blocks_kernel, out_shape=(shape((HEADS, ROWS, nodes), F32)...  11.5 us
    all_to_all x1, starting transfers between devices, local(): lax.all_to_all(outgoing, 'grp', split_axis=0, concat_axis=0, tiled=True)  10.9 us
    pallas_call x1, Pallas kernels, turn_masks(): pl.pallas_call(turn_kernel, out_shape=(jax.ShapeDtypeStruct((hops, planes...  6.57 us
  transfers between devices with their start and end apart: 5, of which 0 were waited for; matrix products, arithmetic and copies ran while one was open for 0% of the time, Pallas kernels for 8%

profile of v1, /device:TPU:1, one launch (start us, length us, event | category | flops | bytes accessed | tf_op | source)
XLA Modules:
  0.0 265.8 jit_solution(3717243640027776507)
XLA Ops:
  0.0 2.0 collective-permute-start.1
  2.0 1.6 collective-permute-start
  3.7 2.2 pick_rows.1
  5.9 0.0 copy-start
  5.9 0.0 copy-start.1
  5.9 0.0 copy-start.2
  5.9 0.0 copy-start.3
  5.9 6.6 %turn_masks.1 = (bf16[3,6,768,128]{3,2,1,0:T(8,128)(2,1)}, bf16[6,512,128]{2,1,0:T(8,128)(2,1)}) custom-call(s32[16]{0:T(128)} %bitcast.10, s32[5,768,768]{2,1,0:T(8,128)} %bitcast.6, s32[768,512]{1,0:T(8,128)} %bound_hbm.1), custom_call_target="tpu_custom_call" | custom-call | tf_op jit(solution)/shard_map/turn_masks/pallas_call | solution.py:174
  12.5 0.0 collective-permute-done.1.x4
  12.5 0.0 collective-permute-done.x2
  12.5 0.0 copy-done
  12.5 1.4 collective-permute-start.2
  13.9 0.1 collective-permute-start.3
  14.0 10.9 %all-to-all-start = ((bf16[16,32,128]{2,1,0:T(8,128)(2,1)}), bf16[16,32,128]{2,1,0:T(8,128)(2,1)S(1)}, u32[]{:S(2)}, u32[]{:S(2)}) async-start(bf16[16,32,128]{2,1,0:T(8,128)(2,1)} %bitcast.3), calls=%async_computation | async-start | bytes 262144 | tf_op jit(solution)/shard_map/all_to_all | solution.py:426
  24.9 0.0 collective-permute-done.2
  24.9 0.0 collective-permute-done.3
  25.0 0.0 copy-done.1
  25.0 0.0 copy-done.2
  25.0 0.0 copy-done.3
  25.0 11.5 %node_blocks.1 = (f32[8,80,768]{2,1,0:T(8,128)S(1)}, f32[8,768]{1,0:T(8,128)S(1)}, f32[8,128]{1,0:T(8,128)S(1)}) custom-call(bf16[768,128]{1,0:T(8,128)(2,1)S(1)} %copy-done, bf16[768,128]{1,0:T(8,128)(2,1)S(1)} %get-tuple-element.22.x1, bf16[768,128]{1,0:T(8,128)(2,1)S(1)} %collective-permute-done.x2, bf16[768,128]{1,0:T(8,128)(2,1)S(1)} %get-tuple-element.21.x3, ...), custom_call_target="tpu_custom_call" | custom-call | tf_op jit(solution)/shard_map/node_blocks/pallas_call | solution.py:280
  36.5 0.0 all-to-all-done
  36.5 229.1 %last_block.1 = bf16[768,512]{1,0:T(8,128)(2,1)} custom-call(bf16[768,128]{1,0:T(8,128)(2,1)S(1)} %copy-done, bf16[768,128]{1,0:T(8,128)(2,1)S(1)} %get-tuple-element.22.x1, bf16[768,128]{1,0:T(8,128)(2,1)S(1)} %collective-permute-done.x2, bf16[768,128]{1,0:T(8,128)(2,1)S(1)} %get-tuple-element.21.x3, bf16[768,128]{1,0:T(8,128)(2,1)S(1)} %collective-permute-done.1.x4, ...), custom_call_target="tpu_custom_call" | custom-call | tf_op jit(solution)/shard_map/last_block/pallas_call | solution.py:385
  (2 shorter events, 0.1 us)
Async XLA Ops:
  0.0 12.5 %collective-permute-start.1 = (bf16[768,128]{1,0:T(8,128)(2,1)}, bf16[768,128]{1,0:T(8,128)(2,1)S(1)}, u32[]{:S(2)}, u32[]{:S(2)}) collective-permute-start(bf16[768,128]{1,0:T(8,128)(2,1)} %x0.3), channel_id=1, source_target_pairs={{12,0},{13,1},{14,2},{15,3},{0,4},{1,5},{2,6},{3,7},{4,8},{5,9},{6... | collective-permute-start | bytes 589832 | tf_op jit(solution)/shard_map/ppermute | solution.py:414
  2.0 10.4 %collective-permute-start = (bf16[768,128]{1,0:T(8,128)(2,1)}, bf16[768,128]{1,0:T(8,128)(2,1)S(1)}, u32[]{:S(2)}, u32[]{:S(2)}) collective-permute-start(bf16[768,128]{1,0:T(8,128)(2,1)} %x0.3), channel_id=1, source_target_pairs={{14,0},{15,1},{0,2},{1,3},{2,4},{3,5},{4,6},{5,7},{6,8},{7,9},{8,1... | collective-permute-start | bytes 589832 | tf_op jit(solution)/shard_map/ppermute | solution.py:414
  5.9 6.6 %copy-start = (bf16[768,128]{1,0:T(8,128)(2,1)S(1)}, bf16[768,128]{1,0:T(8,128)(2,1)}, u32[]{:S(2)}) copy-start(bf16[768,128]{1,0:T(8,128)(2,1)} %x0.3) | copy-start | bytes 589828
  5.9 19.1 %copy-start.1 = (bf16[128,512]{1,0:T(8,128)(2,1)S(1)}, bf16[128,512]{1,0:T(8,128)(2,1)}, u32[]{:S(2)}) copy-start(bf16[128,512]{1,0:T(8,128)(2,1)} %proj_ref.3) | copy-start | bytes 393220
  5.9 19.1 %copy-start.2 = (f32[8,64]{1,0:T(8,128)S(1)}, f32[8,64]{1,0:T(8,128)}, u32[]{:S(2)}) copy-start(f32[8,64]{1,0:T(8,128)} %src_ref.3) | copy-start | bytes 6148
  5.9 19.1 %copy-start.3 = (f32[8,64]{1,0:T(8,128)S(1)}, f32[8,64]{1,0:T(8,128)}, u32[]{:S(2)}) copy-start(f32[8,64]{1,0:T(8,128)} %dst_ref.1) | copy-start | bytes 6148
  12.5 12.4 %collective-permute-start.2 = (bf16[768,128]{1,0:T(8,128)(2,1)S(1)}, bf16[768,128]{1,0:T(8,128)(2,1)S(1)}, u32[]{:S(2)}, u32[]{:S(2)}) collective-permute-start(bf16[768,128]{1,0:T(8,128)(2,1)S(1)} %broadcast_select_fusion.2), channel_id=1, source_target_pairs={{0,1},{1,0},{2,3},{3,2},{4,5},{5,4},{6,7},{7,6},{8,9},{9,8},{10,11... | collective-permute-start | bytes 589832 | tf_op jit(solution)/shard_map/ppermute | solution.py:418
  13.9 11.0 %collective-permute-start.3 = (bf16[768,128]{1,0:T(8,128)(2,1)S(1)}, bf16[768,128]{1,0:T(8,128)(2,1)S(1)}, u32[]{:S(2)}, u32[]{:S(2)}) collective-permute-start(bf16[768,128]{1,0:T(8,128)(2,1)S(1)} %collective-permute-done.x2), channel_id=1, source_target_pairs={{0,1},{1,0},{2,3},{3,2},{4,5},{5,4},{6,7},{7,6},{8,9},{9,8},{10,11... | collective-permute-start | bytes 589832 | tf_op jit(solution)/shard_map/ppermute | solution.py:418
  14.0 22.5 %all-to-all-start = ((bf16[16,32,128]{2,1,0:T(8,128)(2,1)}), bf16[16,32,128]{2,1,0:T(8,128)(2,1)S(1)}, u32[]{:S(2)}, u32[]{:S(2)}) async-start(bf16[16,32,128]{2,1,0:T(8,128)(2,1)} %bitcast.3), calls=%async_computation | async-start | bytes 262144 | tf_op jit(solution)/shard_map/all_to_all | solution.py:426

commit v2 on v1

--- a/solution.py
+++ b/solution.py
@@ -309,7 +309,7 @@
 
     def finish(h, acc):
         o = acc[0:HEAD_DIM] * (1.0 / acc[HEAD_DIM : HEAD_DIM + 1])
-        turned_out[h * HEAD_DIM : (h + 1) * HEAD_DIM, :] = elu(o)
+        turned_out[h * HEAD_DIM : (h + 1) * HEAD_DIM, :] = elu(o).astype(BF16)
 
     @pl.when(worst <= SPAN)
     def _():
@@ -325,7 +325,7 @@
                 for h in range(HEADS):
                     part = weighted(h, range(i * per, (i + 1) * per), table, rise, ratio, mask)
                     finish(h, acc_in[h, :, lanes] + part)
-                out_ref[lanes, :] = turned_out[...].T.astype(BF16)
+                out_ref[lanes, :] = turned_out[...].T
 
         pl.run_scoped(body, *scratch(xs.shape[0], nodes, 1))
 
@@ -376,7 +376,7 @@
             lanes = slice(i * TILE, (i + 1) * TILE)
             for h in range(HEADS):
                 finish(h, sums[h, :, lanes])
-            out_ref[lanes, :] = turned_out[...].T.astype(BF16)
+            out_ref[lanes, :] = turned_out[...].T
 
 
 def last_block(blocks, slots, proj, att_src, dst, worst, acc, bound, edges):
@@ -390,7 +390,7 @@
         scratch_shapes=[
             pltpu.VMEM(bound.shape, BF16),
             pltpu.SemaphoreType.DMA,
-            pltpu.VMEM((width, TILE), F32),
+            pltpu.VMEM((width, TILE), BF16),
             pltpu.VMEM((LANES, nodes), jnp.int32),
             pltpu.VMEM((HEADS, ROWS, nodes), BF16),
             pltpu.VMEM((nodes, HEADS), F32),

time: 268 us -> 268 us (level)
  no operation moved by 1% of the time
where the time goes in v2:
time: 268 us; the launch traced here: 266 us
  Pallas kernels  249 us (93%)
  starting transfers between devices  16.1 us (6%)
    pallas_call x1, Pallas kernels, last_block(): pl.pallas_call(last_kernel, out_shape=jax.ShapeDtypeStruct((nodes, width)...  229 us
    pallas_call x1, Pallas kernels, node_blocks(): pl.pallas_call(blocks_kernel, out_shape=(shape((HEADS, ROWS, nodes), F32)...  11.5 us
    all_to_all x1, starting transfers between devices, local(): lax.all_to_all(outgoing, 'grp', split_axis=0, concat_axis=0, tiled=True)  10.9 us
    pallas_call x1, Pallas kernels, turn_masks(): pl.pallas_call(turn_kernel, out_shape=(jax.ShapeDtypeStruct((hops, planes...  6.57 us
  transfers between devices with their start and end apart: 5, of which 0 were waited for; matrix products, arithmetic and copies ran while one was open for 0% of the time, Pallas kernels for 8%

profile of v2, /device:TPU:1, one launch (start us, length us, event | category | flops | bytes accessed | tf_op | source)
XLA Modules:
  0.0 265.8 jit_solution(16642956872488604475)
XLA Ops:
  0.0 2.0 collective-permute-start.1
  2.0 1.6 collective-permute-start
  3.7 2.2 pick_rows.1
  5.9 0.0 copy-start
  5.9 0.0 copy-start.1
  5.9 0.0 copy-start.2
  5.9 0.0 copy-start.3
  5.9 6.6 %turn_masks.1 = (bf16[3,6,768,128]{3,2,1,0:T(8,128)(2,1)}, bf16[6,512,128]{2,1,0:T(8,128)(2,1)}) custom-call(s32[16]{0:T(128)} %bitcast.10, s32[5,768,768]{2,1,0:T(8,128)} %bitcast.6, s32[768,512]{1,0:T(8,128)} %bound_hbm.1), custom_call_target="tpu_custom_call" | custom-call | tf_op jit(solution)/shard_map/turn_masks/pallas_call | solution.py:174
  12.5 0.0 collective-permute-done.1.x4
  12.5 0.0 collective-permute-done.x2
  12.5 0.0 copy-done
  12.5 1.4 collective-permute-start.2
  13.9 0.1 collective-permute-start.3
  14.0 10.9 %all-to-all-start = ((bf16[16,32,128]{2,1,0:T(8,128)(2,1)}), bf16[16,32,128]{2,1,0:T(8,128)(2,1)S(1)}, u32[]{:S(2)}, u32[]{:S(2)}) async-start(bf16[16,32,128]{2,1,0:T(8,128)(2,1)} %bitcast.3), calls=%async_computation | async-start | bytes 262144 | tf_op jit(solution)/shard_map/all_to_all | solution.py:426
  24.9 0.0 collective-permute-done.2
  24.9 0.0 collective-permute-done.3
  25.0 0.0 copy-done.1
  25.0 0.0 copy-done.2
  25.0 0.0 copy-done.3
  25.0 11.5 %node_blocks.1 = (f32[8,80,768]{2,1,0:T(8,128)S(1)}, f32[8,768]{1,0:T(8,128)S(1)}, f32[8,128]{1,0:T(8,128)S(1)}) custom-call(bf16[768,128]{1,0:T(8,128)(2,1)S(1)} %copy-done, bf16[768,128]{1,0:T(8,128)(2,1)S(1)} %get-tuple-element.22.x1, bf16[768,128]{1,0:T(8,128)(2,1)S(1)} %collective-permute-done.x2, bf16[768,128]{1,0:T(8,128)(2,1)S(1)} %get-tuple-element.21.x3, ...), custom_call_target="tpu_custom_call" | custom-call | tf_op jit(solution)/shard_map/node_blocks/pallas_call | solution.py:280
  36.5 0.0 all-to-all-done
  36.5 229.1 %last_block.1 = bf16[768,512]{1,0:T(8,128)(2,1)} custom-call(bf16[768,128]{1,0:T(8,128)(2,1)S(1)} %copy-done, bf16[768,128]{1,0:T(8,128)(2,1)S(1)} %get-tuple-element.22.x1, bf16[768,128]{1,0:T(8,128)(2,1)S(1)} %collective-permute-done.x2, bf16[768,128]{1,0:T(8,128)(2,1)S(1)} %get-tuple-element.21.x3, bf16[768,128]{1,0:T(8,128)(2,1)S(1)} %collective-permute-done.1.x4, ...), custom_call_target="tpu_custom_call" | custom-call | tf_op jit(solution)/shard_map/last_block/pallas_call | solution.py:385
  (2 shorter events, 0.1 us)
Async XLA Ops:
  0.0 12.5 %collective-permute-start.1 = (bf16[768,128]{1,0:T(8,128)(2,1)}, bf16[768,128]{1,0:T(8,128)(2,1)S(1)}, u32[]{:S(2)}, u32[]{:S(2)}) collective-permute-start(bf16[768,128]{1,0:T(8,128)(2,1)} %x0.3), channel_id=1, source_target_pairs={{12,0},{13,1},{14,2},{15,3},{0,4},{1,5},{2,6},{3,7},{4,8},{5,9},{6... | collective-permute-start | bytes 589832 | tf_op jit(solution)/shard_map/ppermute | solution.py:414
  2.0 10.4 %collective-permute-start = (bf16[768,128]{1,0:T(8,128)(2,1)}, bf16[768,128]{1,0:T(8,128)(2,1)S(1)}, u32[]{:S(2)}, u32[]{:S(2)}) collective-permute-start(bf16[768,128]{1,0:T(8,128)(2,1)} %x0.3), channel_id=1, source_target_pairs={{14,0},{15,1},{0,2},{1,3},{2,4},{3,5},{4,6},{5,7},{6,8},{7,9},{8,1... | collective-permute-start | bytes 589832 | tf_op jit(solution)/shard_map/ppermute | solution.py:414
  5.9 6.6 %copy-start = (bf16[768,128]{1,0:T(8,128)(2,1)S(1)}, bf16[768,128]{1,0:T(8,128)(2,1)}, u32[]{:S(2)}) copy-start(bf16[768,128]{1,0:T(8,128)(2,1)} %x0.3) | copy-start | bytes 589828
  5.9 19.1 %copy-start.1 = (bf16[128,512]{1,0:T(8,128)(2,1)S(1)}, bf16[128,512]{1,0:T(8,128)(2,1)}, u32[]{:S(2)}) copy-start(bf16[128,512]{1,0:T(8,128)(2,1)} %proj_ref.3) | copy-start | bytes 393220
  5.9 19.1 %copy-start.2 = (f32[8,64]{1,0:T(8,128)S(1)}, f32[8,64]{1,0:T(8,128)}, u32[]{:S(2)}) copy-start(f32[8,64]{1,0:T(8,128)} %src_ref.3) | copy-start | bytes 6148
  5.9 19.1 %copy-start.3 = (f32[8,64]{1,0:T(8,128)S(1)}, f32[8,64]{1,0:T(8,128)}, u32[]{:S(2)}) copy-start(f32[8,64]{1,0:T(8,128)} %dst_ref.1) | copy-start | bytes 6148
  12.5 12.4 %collective-permute-start.2 = (bf16[768,128]{1,0:T(8,128)(2,1)S(1)}, bf16[768,128]{1,0:T(8,128)(2,1)S(1)}, u32[]{:S(2)}, u32[]{:S(2)}) collective-permute-start(bf16[768,128]{1,0:T(8,128)(2,1)S(1)} %broadcast_select_fusion.2), channel_id=1, source_target_pairs={{0,1},{1,0},{2,3},{3,2},{4,5},{5,4},{6,7},{7,6},{8,9},{9,8},{10,11... | collective-permute-start | bytes 589832 | tf_op jit(solution)/shard_map/ppermute | solution.py:418
  13.9 11.0 %collective-permute-start.3 = (bf16[768,128]{1,0:T(8,128)(2,1)S(1)}, bf16[768,128]{1,0:T(8,128)(2,1)S(1)}, u32[]{:S(2)}, u32[]{:S(2)}) collective-permute-start(bf16[768,128]{1,0:T(8,128)(2,1)S(1)} %collective-permute-done.x2), channel_id=1, source_target_pairs={{0,1},{1,0},{2,3},{3,2},{4,5},{5,4},{6,7},{7,6},{8,9},{9,8},{10,11... | collective-permute-start | bytes 589832 | tf_op jit(solution)/shard_map/ppermute | solution.py:418
  14.0 22.5 %all-to-all-start = ((bf16[16,32,128]{2,1,0:T(8,128)(2,1)}), bf16[16,32,128]{2,1,0:T(8,128)(2,1)S(1)}, u32[]{:S(2)}, u32[]{:S(2)}) async-start(bf16[16,32,128]{2,1,0:T(8,128)(2,1)} %bitcast.3), calls=%async_computation | async-start | bytes 262144 | tf_op jit(solution)/shard_map/all_to_all | solution.py:426
